TPU v7x, 32 devices: a whole 2x2x4 slice. The times are simulated.
32 devices in a mesh: dp: 8 (over z, x), segment: 2 (over y), mp: 2 (over core).
Axes of the slice: x: 2, y: 2, z: 4, core: 2. Of those that a mesh axis runs over, the one named last changes fastest.
Arguments:
- prefix_hidden: bfloat16 [16, 512, 8192], P(('dp', 'segment'), 'mp'), may hold values from -6 to 6
- norm_gain: float32 [8192], replicated, may hold values from 0.5 to 1.5
- kv_weight: bfloat16 [8192, 2, 1024], P('dp', None, 'mp'), may hold values from -0.0625 to 0.0625
- action_query: bfloat16 [16, 128, 2048], P(('dp', 'segment'), None, 'mp'), may hold values from -104 to 104
- action_kv: bfloat16 [16, 128, 2, 1024], P(('dp', 'segment'), None, None, 'mp'), may hold values from -4.25 to 4.25
- out_cotangent: bfloat16 [16, 128, 2048], P(('dp', 'segment'), None, 'mp'), may hold values from -18 to 18
- prefix_blocks: int32 [16, 512], P(('dp', 'segment')), may hold values from 0 to 7, as said below
- action_blocks: int32 [16, 128], P(('dp', 'segment')), may hold values from 0 to 8, as said below
- prefix_lengths: int32 [16], P(('dp', 'segment')), may hold values from 128 to 512, as said below
- timesteps: int32 [16], P(('dp', 'segment')), may hold values from 0 to 999
Outputs:
- attn_out: bfloat16 [16, 128, 2048], P(('dp', 'segment'), None, 'mp')
- query_grad: float32 [16, 128, 2048], P(('dp', 'segment'), None, 'mp')
- action_kv_grad: float32 [16, 128, 2, 1024], P(('dp', 'segment'), None, None, 'mp')
- weight_grad: float32 [8192, 2, 1024], P('dp', None, 'mp')
Inputs may be any that keep to these rules, and one draw needn't show every extreme that they name: `prefix_blocks`: constant over each run of 64 positions, 0 on the first run, rising by 0 or 1 from one run to the next; in every draw some sample rises at every run. `action_blocks`: constant over each run of 64 positions; the last run of every sample holds 8; in every draw some sample's first run holds 0. `prefix_lengths`: in every draw some sample's prefix is whole and some sample's is 128.
All inputs are finite; a program needn't handle non-finite values.
Results may differ from a plain program's by a relative error of at most 0.017.
Values may be sent and summed in bfloat16 or wider, within the bound.
A program may use at most 128 MiB of HBM per device.

v0:
```python
import jax
import jax.numpy as jnp
from jax import lax
from jax.sharding import PartitionSpec as P

KVH = 8
HD = 128
QH = 16
STEPS = 1000
EPS = 1e-06
NEGATIVE = -1e30


def head_scores(query, keys):
    return jnp.einsum("agrh,jgh->graj", query, keys, preferred_element_type=jnp.float32) * HD ** (
        -0.5
    )


def backward_terms(probs, values, keys, query, grad_out):
    probs_low = probs.astype(jnp.bfloat16)
    d_probs = jnp.einsum("agrh,jgh->graj", grad_out, values, preferred_element_type=jnp.float32)
    delta = jnp.sum(probs * d_probs, axis=-1, keepdims=True)
    d_scores = (probs * (d_probs - delta)).astype(jnp.bfloat16)
    d_query = jnp.einsum(
        "graj,jgh->agrh", d_scores, keys, preferred_element_type=jnp.float32
    ) * HD ** (-0.5)
    d_keys = jnp.einsum(
        "graj,agrh->jgh", d_scores, query, preferred_element_type=jnp.float32
    ) * HD ** (-0.5)
    d_values = jnp.einsum("graj,agrh->jgh", probs_low, grad_out, preferred_element_type=jnp.float32)
    return (d_query, jnp.stack([d_keys, d_values], axis=1))


def shards(
    prefix_hidden,
    norm_gain,
    kv_weight,
    action_query,
    action_kv,
    out_cotangent,
    prefix_blocks,
    action_blocks,
    prefix_lengths,
    timesteps,
):
    acts = action_query.shape[1]
    heads_kv = kv_weight.shape[2] // HD
    ratio = QH // KVH
    columns = 2 * kv_weight.shape[2]
    wide = prefix_hidden[0].astype(jnp.float32)
    inverse = lax.rsqrt(jnp.mean(wide * wide, axis=-1, keepdims=True) + EPS)
    normed_local = (wide * inverse * norm_gain).astype(jnp.bfloat16)
    normed = lax.all_gather(normed_local, "mp", axis=0, tiled=True)
    rows = normed.shape[0]
    piece = lax.all_gather(kv_weight, "dp", axis=0, tiled=True)
    section = normed
    projected = jnp.dot(
        section, piece.reshape(piece.shape[0], columns), preferred_element_type=jnp.float32
    )
    prefix_kv = projected.astype(jnp.bfloat16).reshape(rows, 2, heads_kv, HD)
    own_pair = action_kv[0].reshape(acts, 2, heads_kv, HD)
    query = action_query[0].reshape(acts, heads_kv, ratio, HD)
    flow_weight = 0.5 + (timesteps[0].astype(jnp.float32) + 0.5) / STEPS
    grad_out = (
        (flow_weight * out_cotangent[0].astype(jnp.float32))
        .astype(jnp.bfloat16)
        .reshape(acts, heads_kv, ratio, HD)
    )
    pblocks = prefix_blocks[0]
    ablocks = action_blocks[0]
    length = prefix_lengths[0]
    keys = jnp.concatenate([prefix_kv[:, 0], own_pair[:, 0]], axis=0)
    values = jnp.concatenate([prefix_kv[:, 1], own_pair[:, 1]], axis=0)
    positions = jnp.arange(rows, dtype=jnp.int32)
    see_prefix = (pblocks[None, :] <= ablocks[:, None]) & (positions[None, :] < length)
    see_action = ablocks[None, :] <= ablocks[:, None]
    visible = jnp.concatenate([see_prefix, see_action], axis=1)
    masked = jnp.where(visible, head_scores(query, keys), NEGATIVE)
    top = jnp.max(masked, axis=-1, keepdims=True)
    expo = jnp.where(visible, jnp.exp(masked - top), 0.0)
    probs = expo / jnp.sum(expo, axis=-1, keepdims=True)
    out = jnp.einsum(
        "graj,jgh->agrh", probs.astype(jnp.bfloat16), values, preferred_element_type=jnp.float32
    )
    d_query, d_pair = backward_terms(probs, values, keys, query, grad_out)
    d_prefix = d_pair[:rows]
    d_action = d_pair[rows:]
    attn_out = out.astype(jnp.bfloat16).reshape(1, acts, ratio * heads_kv * HD)
    query_grad = d_query.reshape(1, acts, ratio * heads_kv * HD)
    action_kv_grad = d_action.reshape(1, acts, 2, heads_kv * HD)
    prefix_grad = d_prefix.astype(jnp.bfloat16).reshape(rows, columns)
    section = normed
    term = lax.dot_general(
        section, prefix_grad, (((0,), (0,)), ((), ())), preferred_element_type=jnp.float32
    )
    shard = lax.psum_scatter(
        term.reshape(kv_weight.shape[0] * lax.axis_size("dp"), 2, columns // 2).astype(
            jnp.bfloat16
        ),
        "dp",
        scatter_dimension=0,
        tiled=True,
    )
    weight_grad = lax.psum(shard, "segment").astype(jnp.float32)
    return (attn_out, query_grad, action_kv_grad, weight_grad)


def solution(mesh):
    placed = (
        P(("dp", "segment"), "mp", None),
        P(),
        P("dp", None, "mp"),
        P(("dp", "segment"), None, "mp"),
        P(("dp", "segment"), None, None, "mp"),
        P(("dp", "segment"), None, "mp"),
        P(("dp", "segment"), None),
        P(("dp", "segment"), None),
        P(("dp", "segment")),
        P(("dp", "segment")),
    )
    return jax.shard_map(
        shards,
        mesh=mesh,
        in_specs=placed,
        out_specs=(
            P(("dp", "segment"), None, "mp"),
            P(("dp", "segment"), None, "mp"),
            P(("dp", "segment"), None, None, "mp"),
            P("dp", None, "mp"),
        ),
        check_vma=False,
    )
```

profile of v0, /device:TPU:0, one launch (start us, length us, event | category | flops | bytes accessed | tf_op | source)
XLA Modules:
  0.0 657.0 jit_solution(16205726771575805277)
XLA Ops:
  7.2 0.0 all-gather.5.cloned.1.call-start
  7.2 0.7 all-gather.5.cloned.1.call-update
  7.9 0.0 all-gather.3.cloned.1.call-start
  8.0 6.4 copy.51
  14.3 3.5 fusion.1
  17.8 2.6 fusion.3
  20.5 0.0 copy-start.11
  20.5 0.0 all-gather.3.cloned.1.call-update
  20.5 0.0 reduce-scatter.2.cloned.1.call-start
  22.0 0.8 copy.88
  22.9 0.2 copy.87
  23.1 0.2 copy.53
  23.3 0.7 fusion.29
  24.0 0.1 copy.86
  24.1 0.1 broadcast_compare_fusion
  24.2 0.2 compare_and_fusion
  24.4 0.6 pad_add_fusion
  25.1 215.0 %all-gather.5.cloned.1.call-done = bf16[8192,2,512]{2,1,0:T(2,128)(2,1)} async-done(((bf16[1024,2,512]{2,1,0:T(2,128)(2,1)}), bf16[8192,2,512]{2,1,0:T(2,128)(2,1)}) %all-gather.5.cloned.1.call-update) | async-done | bytes 16777232 | tf_op jit(solution)/shard_map/all_gather | solution.py:56
  240.1 17.3 %copy.89 = bf16[1024,8,2,512]{3,1,2,0:T(8,128)(2,1)} copy(bf16[1024,8,2,512]{3,2,1,0:T(2,128)(2,1)} %bitcast.107) | data formatting | bytes 33554432
  257.5 1.1 all-gather.3.cloned.1.call-done
  258.5 14.8 %convolution_convert_fusion.1 = bf16[512,1024]{1,0:T(8,128)(2,1)S(1)} fusion(bf16[512,8192]{0,1:T(8,128)(2,1)} %all-gather.3.cloned.1.call-done, bf16[8192,1024]{1,0:T(8,128)(2,1)} %bitcast.108), kind=kOutput, calls=%fused_computation.20 | convolution fusion | flops 8590458880 | bytes 26214400 | tf_op jit(solution)/shard_map/dot_general | solution.py:58
  273.4 0.8 reshape.62
  274.2 0.4 fusion.28
  274.5 0.1 copy.91
  274.6 1.1 copy.84
  275.7 2.1 fusion.30
  277.9 0.0 copy-start.3
  277.9 0.0 copy-start.7
  277.9 1.8 convolution_bitcast_fusion
  279.7 0.1 copy-done.7
  279.8 0.1 copy-done.8
  279.9 0.6 fusion.5
  280.5 2.2 fusion.7
  282.7 0.5 fusion.11
  283.3 0.2 fusion.8
  283.4 16.1 %convolution_convert_fusion = bf16[8192,2,512]{2,0,1:T(8,128)(2,1)} fusion(bf16[2,512,512]{2,1,0:T(8,128)(2,1)S(1)} %bitcast.113, bf16[512,8192]{0,1:T(8,128)(2,1)} %all-gather.3.cloned.1.call-done), kind=kOutput, calls=%fused_computation.1 | convolution fusion | flops 8598323200 | bytes 26214400 | tf_op jit(solution)/shard_map/dot_general | solution.py:94
  299.5 0.0 reduce-scatter.2.cloned.1.call-update
  299.5 0.0 all-reduce.2.cloned.1.call-start
  299.6 280.8 %reduce-scatter.2.cloned.1.call-done = bf16[1024,2,512]{2,0,1:T(8,128)(2,1)} async-done(((bf16[8192,2,512]{2,0,1:T(8,128)(2,1)}), bf16[1024,2,512]{2,0,1:T(8,128)(2,1)}) %reduce-scatter.2.cloned.1.call-update) | async-done | bytes 2097168 | tf_op jit(solution)/shard_map/reduce_scatter | solution.py:97
  580.4 0.0 all-reduce.2.cloned.1.call-update
  580.5 2.3 convolution_convert_fusion.2
  582.8 0.9 copy.66
  583.6 1.2 convolution_multiply_fusion
  584.9 2.0 copy.67
  586.9 1.0 fusion.17
  588.0 1.0 copy.68
  589.0 55.8 %all-reduce.2.cloned.1.call-done = bf16[1024,2,512]{2,0,1:T(8,128)(2,1)} async-done(((bf16[1024,2,512]{2,0,1:T(8,128)(2,1)}), bf16[1024,2,512]{2,0,1:T(8,128)(2,1)}) %all-reduce.2.cloned.1.call-update) | async-done | bytes 2097168 | tf_op jit(solution)/shard_map/psum | solution.py:105
  644.7 5.8 copy.69
  (22 shorter events, 0.1 us)
Async XLA Ops:
  7.2 233.0 %all-gather.5.cloned.1.call-start = ((), (), s32[]{:S(2)}) async-start(), calls=%async_computation.2 | async-start | bytes 18874368 | tf_op jit(solution)/shard_map/all_gather | solution.py:56
  7.9 250.6 %all-gather.3.cloned.1.call-start = ((), (), s32[]{:S(2)}) async-start(), calls=%async_computation.1 | async-start | bytes 12582912 | tf_op jit(solution)/shard_map/all_gather | solution.py:54
  7.9 9.8 %copy-start.9 = (f32[8192]{0:T(1024)S(1)}, f32[8192]{0:T(1024)}, u32[]{:S(2)}) copy-start(f32[8192]{0:T(1024)} %param.11) | copy-start | bytes 98308
  14.3 3.5 copy-start
  20.4 1.5 copy-start.4
  20.4 2.4 copy-start.5
  20.4 2.6 copy-start.6
  20.4 3.7 copy-start.10
  20.5 3.8 copy-start.11
  20.5 559.9 %reduce-scatter.2.cloned.1.call-start = ((), (), s32[]{:S(2)}) async-start(), calls=%async_computation.3 | async-start | bytes 18874368 | tf_op jit(solution)/shard_map/reduce_scatter | solution.py:97
  277.9 1.9 copy-start.2
  277.9 1.9 copy-start.3
  277.9 1.9 copy-start.7
  277.9 2.0 copy-start.8
  279.7 3.5 copy-start.1
  299.5 345.2 %all-reduce.2.cloned.1.call-start = ((), (), s32[]{:S(2)}) async-start(), calls=%async_computation.4 | async-start | bytes 4194304 | tf_op jit(solution)/shard_map/psum | solution.py:105
Sparse Core Ops, SparseCore 0:
  10.1 229.9 all-gather.4
  242.2 16.2 all-gather.2
  299.7 280.7 reduce-scatter.1
  582.6 62.1 all-reduce.1
where the time goes:
time: 658 us; the launch traced here: 657 us
  waiting for transfers between devices  553 us (84%)
  matrix products  39.5 us (6%)
  local copies, waits for them, and re-layouts  38 us (6%)
  between operations  15.4 us (2%)
  other arithmetic  10.5 us (2%)
    reduce_scatter x1, waiting for transfers between devices, shards(): lax.psum_scatter(term.reshape(kv_weight.shape[0] * lax.axis_size('dp'), 2...  281 us
    all_gather x1, waiting for transfers between devices, shards(): piece = lax.all_gather(kv_weight, 'dp', axis=0, tiled=True)  215 us
    psum x1, waiting for transfers between devices, shards(): weight_grad = lax.psum(shard, 'segment').astype(jnp.float32)  55.8 us
    unnamed x34, local copies, waits for them, and re-layouts  35.1 us
    dot_general x1, matrix products, shards(): lax.dot_general(section, prefix_grad, (((0,), (0,)), ((), ())), preferred...  16.1 us
    dot_general x1, matrix products, shards(): jnp.dot(section, piece.reshape(piece.shape[0], columns), preferred_elemen...  14.8 us
  transfers between devices with their start and end apart: 4, of which 4 were waited for; matrix products, arithmetic and copies ran while one was open for 6% of the time, Pallas kernels for 0%

commit v1 on v0

--- a/solution.py
+++ b/solution.py
@@ -102,7 +102,7 @@
         scatter_dimension=0,
         tiled=True,
     )
-    weight_grad = lax.psum(shard, "segment").astype(jnp.float32)
+    weight_grad = (shard + lax.ppermute(shard, "segment", [(0, 1), (1, 0)])).astype(jnp.float32)
     return (attn_out, query_grad, action_kv_grad, weight_grad)
 
 

time: 658 us -> 642 us (0.976)
  waiting for transfers between devices: 553 us -> 535 us
    psum x1 -> x0, waiting for transfers between devices: 55.8 us -> none  [shards(): weight_grad = lax.psum(shard, 'segment').astype(jnp.float32)]
    ppermute x0 -> x1, waiting for transfers between devices: none -> 37.2 us  [shards(): lax.ppermute(shard, 'segment', [(0, 1), (1, 0)])]
where the time goes in v1:
time: 642 us
  waiting for transfers between devices  535 us (83%)
  matrix products  39.6 us (6%)
  local copies, waits for them, and re-layouts  37.4 us (6%)
  between operations  15.4 us (2%)
  other arithmetic  12.9 us (2%)
    reduce_scatter x1, waiting for transfers between devices, shards(): lax.psum_scatter(term.reshape(kv_weight.shape[0] * lax.axis_size('dp'), 2...  281 us
    all_gather x1, waiting for transfers between devices, shards(): piece = lax.all_gather(kv_weight, 'dp', axis=0, tiled=True)  215 us
    ppermute x1, waiting for transfers between devices, shards(): lax.ppermute(shard, 'segment', [(0, 1), (1, 0)])  37.2 us
    unnamed x34, local copies, waits for them, and re-layouts  34.6 us
    dot_general x1, matrix products, shards(): lax.dot_general(section, prefix_grad, (((0,), (0,)), ((), ())), preferred...  16.1 us
    dot_general x1, matrix products, shards(): jnp.dot(section, piece.reshape(piece.shape[0], columns), preferred_elemen...  14.9 us
  transfers between devices with their start and end apart: 4, of which 4 were waited for; matrix products, arithmetic and copies ran while one was open for 6% of the time, Pallas kernels for 0%

profile of v1, /device:TPU:0, one launch (start us, length us, event | category | flops | bytes accessed | tf_op | source)
XLA Modules:
  0.0 641.8 jit_solution(12233328159375121795)
XLA Ops:
  7.2 0.0 all-gather.5.cloned.1.call-start
  7.2 0.7 all-gather.5.cloned.1.call-update
  7.9 0.0 all-gather.3.cloned.1.call-start
  8.0 6.4 copy.51
  14.3 3.5 fusion.1
  17.8 2.6 fusion.3
  20.5 0.0 copy-start.11
  20.5 0.0 all-gather.3.cloned.1.call-update
  20.5 0.0 reduce-scatter.2.cloned.1.call-start
  22.0 0.8 copy.88
  22.9 0.2 copy.87
  23.1 0.2 copy.53
  23.3 0.7 fusion.29
  24.0 0.1 copy.86
  24.1 0.1 broadcast_compare_fusion
  24.2 0.2 compare_and_fusion
  24.4 0.6 pad_add_fusion
  25.1 215.0 %all-gather.5.cloned.1.call-done = bf16[8192,2,512]{2,1,0:T(2,128)(2,1)} async-done(((bf16[1024,2,512]{2,1,0:T(2,128)(2,1)}), bf16[8192,2,512]{2,1,0:T(2,128)(2,1)}) %all-gather.5.cloned.1.call-update) | async-done | bytes 16777232 | tf_op jit(solution)/shard_map/all_gather | solution.py:56
  240.1 17.3 %copy.89 = bf16[1024,8,2,512]{3,1,2,0:T(8,128)(2,1)} copy(bf16[1024,8,2,512]{3,2,1,0:T(2,128)(2,1)} %bitcast.107) | data formatting | bytes 33554432
  257.5 1.1 all-gather.3.cloned.1.call-done
  258.5 14.9 %convolution_convert_fusion.1 = bf16[512,1024]{1,0:T(8,128)(2,1)S(1)} fusion(bf16[512,8192]{0,1:T(8,128)(2,1)} %all-gather.3.cloned.1.call-done, bf16[8192,1024]{1,0:T(8,128)(2,1)} %bitcast.108), kind=kOutput, calls=%fused_computation.21 | convolution fusion | flops 8590458880 | bytes 26214400 | tf_op jit(solution)/shard_map/dot_general | solution.py:58
  273.4 0.8 reshape.62
  274.2 0.4 fusion.28
  274.5 0.1 copy.91
  274.6 1.1 copy.84
  275.7 2.1 fusion.30
  277.9 0.0 copy-start.3
  277.9 0.0 copy-start.7
  277.9 1.8 convolution_bitcast_fusion
  279.8 0.1 copy-done.7
  279.8 0.1 copy-done.8
  280.0 0.6 fusion.5
  280.6 2.2 fusion.7
  282.7 0.5 fusion.11
  283.3 0.2 fusion.8
  283.4 16.1 %convolution_convert_fusion = bf16[8192,2,512]{2,0,1:T(8,128)(2,1)} fusion(bf16[2,512,512]{2,1,0:T(8,128)(2,1)S(1)} %bitcast.113, bf16[512,8192]{0,1:T(8,128)(2,1)} %all-gather.3.cloned.1.call-done), kind=kOutput, calls=%fused_computation.1 | convolution fusion | flops 8598323200 | bytes 26214400 | tf_op jit(solution)/shard_map/dot_general | solution.py:94
  299.6 0.0 reduce-scatter.2.cloned.1.call-update
  299.6 280.8 %reduce-scatter.2.cloned.1.call-done = bf16[1024,2,512]{2,0,1:T(8,128)(2,1)} async-done(((bf16[8192,2,512]{2,0,1:T(8,128)(2,1)}), bf16[1024,2,512]{2,0,1:T(8,128)(2,1)}) %reduce-scatter.2.cloned.1.call-update) | async-done | bytes 2097168 | tf_op jit(solution)/shard_map/reduce_scatter | solution.py:97
  580.4 1.5 collective-permute-start
  581.9 2.3 convolution_convert_fusion.2
  584.2 0.9 copy.66
  585.1 1.2 convolution_multiply_fusion
  586.3 2.0 copy.67
  588.3 1.0 fusion.17
  589.3 1.0 copy.68
  590.3 37.2 %collective-permute-done = bf16[1024,2,512]{2,0,1:T(8,128)(2,1)} collective-permute-done((bf16[1024,2,512]{2,0,1:T(8,128)(2,1)}, bf16[1024,2,512]{2,0,1:T(8,128)(2,1)}, u32[]{:S(2)}, u32[]{:S(2)}) %collective-permute-start) | collective-permute-done | bytes 2097184 | tf_op jit(solution)/shard_map/ppermute | solution.py:105
  627.5 2.5 add_convert_fusion
  630.0 5.2 copy.69
  (22 shorter events, 0.1 us)
Async XLA Ops:
  7.2 233.0 %all-gather.5.cloned.1.call-start = ((), (), s32[]{:S(2)}) async-start(), calls=%async_computation.2 | async-start | bytes 18874368 | tf_op jit(solution)/shard_map/all_gather | solution.py:56
  7.9 250.6 %all-gather.3.cloned.1.call-start = ((), (), s32[]{:S(2)}) async-start(), calls=%async_computation.1 | async-start | bytes 12582912 | tf_op jit(solution)/shard_map/all_gather | solution.py:54
  7.9 9.8 %copy-start.9 = (f32[8192]{0:T(1024)S(1)}, f32[8192]{0:T(1024)}, u32[]{:S(2)}) copy-start(f32[8192]{0:T(1024)} %param.11) | copy-start | bytes 98308
  14.3 3.5 copy-start
  20.4 1.5 copy-start.4
  20.4 2.4 copy-start.5
  20.4 2.6 copy-start.6
  20.4 3.7 copy-start.10
  20.5 3.8 copy-start.11
  20.5 559.9 %reduce-scatter.2.cloned.1.call-start = ((), (), s32[]{:S(2)}) async-start(), calls=%async_computation.3 | async-start | bytes 18874368 | tf_op jit(solution)/shard_map/reduce_scatter | solution.py:97
  277.9 1.9 copy-start.2
  277.9 1.9 copy-start.3
  277.9 1.9 copy-start.7
  277.9 2.0 copy-start.8
  279.7 3.5 copy-start.1
  580.4 47.1 %collective-permute-start = (bf16[1024,2,512]{2,0,1:T(8,128)(2,1)}, bf16[1024,2,512]{2,0,1:T(8,128)(2,1)}, u32[]{:S(2)}, u32[]{:S(2)}) collective-permute-start(bf16[1024,2,512]{2,0,1:T(8,128)(2,1)} %reduce-scatter.2.cloned.1.call-done), channel_id=1, source_target_pairs={{0,2},{2,0},{1,3},{3,1},{4,6},{6,4},{5,7},{7,5},{8,10},{10,8},{9,1... | collective-permute-start | bytes 6291464 | tf_op jit(solution)/shard_map/ppermute | solution.py:105
Sparse Core Ops, SparseCore 0:
  10.1 229.9 all-gather.4
  242.2 16.2 all-gather.2
  299.7 280.6 reduce-scatter.1
